TPU v7x, 32 devices: a whole 2x2x4 slice. The times are simulated.
32 devices in a mesh: dp: 8 (over y, x, core), mp: 4 (over z).
Axes of the slice: x: 2, y: 2, z: 4, core: 2. Of those that a mesh axis runs over, the one named last changes fastest.
Arguments:
- pooled: bfloat16 [2048, 3584], P('dp', 'mp'), may hold values from -4 to 4
- w_out: bfloat16 [3584, 3584], P('mp'), may hold values from -0.028931878 to 0.028931878
- assignments: int32 [2048], P('dp'), may hold values from 0 to 4095
- ema_sums: float32 [4096, 3584], P('mp', 'dp'), may hold values from -0.40089186 to 0.40089186
- ema_counts: float32 [4096], P('mp'), may hold values from 1 to 8
Outputs:
- distances: float32 [2048, 4096], P('dp', 'mp')
- new_sums: float32 [4096, 3584], P('mp', 'dp')
- new_counts: float32 [4096], P('mp')
- new_centroids: bfloat16 [4096, 3584], P('mp', 'dp')
All inputs are finite; a program needn't handle non-finite values.
Results may differ from a plain program's by a relative error of at most 0.0011.
Values may be sent and summed in bfloat16 or wider, within the bound.
A program may use at most 64 MiB of HBM per device.

v0:
```python
import math

import jax
import jax.numpy as jnp
from jax import lax
from jax.sharding import PartitionSpec as P

EPSILON = 1e-06
EMA_DECAY = 0.9


def body(pooled, w_out, assignments, ema_sums, ema_counts):
    partial_value = jnp.dot(pooled, w_out, preferred_element_type=jnp.float32)
    projected = lax.psum(partial_value, "mp")
    inverse_norm = 1.0 / jnp.sqrt(jnp.sum(projected * projected, axis=1, keepdims=True) + EPSILON)
    embedded = (projected * inverse_norm).astype(jnp.bfloat16)
    local_centers = ema_sums.shape[0]
    doc_rows = embedded.shape[0]
    centers = (ema_sums / ema_counts[:, None]).astype(jnp.bfloat16)
    column_piece = lax.all_gather(centers, "dp", axis=1, tiled=True)
    products = lax.dot_general(
        embedded, column_piece, (((1,), (1,)), ((), ())), preferred_element_type=jnp.float32
    )
    piece_wide = column_piece.astype(jnp.float32)
    center_norms = jnp.sum(piece_wide * piece_wide, axis=1)
    products, center_norms = (products, center_norms)
    embed_wide = embedded.astype(jnp.float32)
    doc_norms = jnp.sum(embed_wide * embed_wide, axis=1)
    distances = doc_norms[:, None] + center_norms[None, :] - 2.0 * products
    first_center = lax.axis_index("mp") * local_centers
    center_ids = first_center + jnp.arange(local_centers, dtype=jnp.int32)
    feature_cols = ema_sums.shape[1]
    every_assign = lax.all_gather(assignments, "dp", axis=0, tiled=True)
    own_columns = lax.all_to_all(embedded, "dp", split_axis=1, concat_axis=0, tiled=True)
    shard_count = lax.axis_size("dp")
    group_size = math.gcd(shard_count, max(1, 2048 // doc_rows))
    block_rows = group_size * doc_rows
    turns = shard_count // group_size

    def add_block(block_index, totals):
        sums_now, counts_now = totals
        block_assign = lax.dynamic_slice_in_dim(
            every_assign, block_index * block_rows, block_rows, 0
        )
        block_columns = lax.dynamic_slice_in_dim(
            own_columns, block_index * block_rows, block_rows, 0
        )
        one_hot = (block_assign[None, :] == center_ids[:, None]).astype(jnp.bfloat16)
        sums_now = sums_now + jnp.dot(one_hot, block_columns, preferred_element_type=jnp.float32)
        counts_now = counts_now + jnp.sum(one_hot, axis=1, dtype=jnp.float32)
        return (sums_now, counts_now)

    start_sums = (
        jnp.zeros((local_centers, feature_cols), jnp.float32),
        jnp.zeros((local_centers,), jnp.float32),
    )
    batch_sums, batch_counts = lax.fori_loop(0, turns, add_block, start_sums)
    new_counts = EMA_DECAY * ema_counts + (1.0 - EMA_DECAY) * batch_counts
    new_sums = EMA_DECAY * ema_sums + (1.0 - EMA_DECAY) * batch_sums
    new_centroids = (new_sums / new_counts[:, None]).astype(jnp.bfloat16)
    return (distances, new_sums, new_counts, new_centroids)


def solution(mesh):
    return jax.shard_map(
        body,
        mesh=mesh,
        in_specs=(P("dp", "mp"), P("mp", None), P("dp"), P("mp", "dp"), P("mp")),
        out_specs=(P("dp", "mp"), P("mp", "dp"), P("mp"), P("mp", "dp")),
        check_vma=False,
    )
```

profile of v0, /device:TPU:0, one launch (start us, length us, event | category | flops | bytes accessed | tf_op | source)
XLA Modules:
  0.0 215.6 jit_solution(4043559094026590558)
XLA Ops:
  8.0 0.0 copy-start
  8.0 0.0 all-reduce.2.cloned.1.call-start
  8.1 1.0 copy-done
  9.0 6.8 %fusion.7 = f32[256,3584]{1,0:T(8,128)} fusion(bf16[256,896]{1,0:T(8,128)(2,1)S(1)} %copy-done, bf16[896,3584]{1,0:T(8,128)(2,1)} %param.6), kind=kOutput, calls=%fused_computation.18 | convolution fusion | flops 1644167168 | bytes 10551296 | tf_op jit(solution)/shard_map/dot_general | solution.py:13
  15.8 0.0 copy-start.5
  15.8 0.0 all-reduce.2.cloned.1.call-update
  15.8 0.0 all-gather.3.cloned.1.call-start
  15.9 1.4 copy-done.5
  17.3 0.0 copy-done.7
  17.3 1.1 divide_convert_fusion.1
  18.5 0.0 all-gather.3.cloned.1.call-update
  18.5 138.3 %all-reduce.2.cloned.1.call-done = f32[256,3584]{1,0:T(8,128)} async-done(((f32[256,3584]{1,0:T(8,128)}), f32[256,3584]{1,0:T(8,128)}) %all-reduce.2.cloned.1.call-update) | async-done | bytes 3670032 | tf_op jit(solution)/shard_map/psum | solution.py:14
  156.7 2.5 %multiply_reduce_fusion.2 = f32[256]{0:T(256)S(1)} fusion(f32[256,3584]{1,0:T(8,128)} %all-reduce.2.cloned.1.call-done), kind=kLoop, calls=%fused_computation.9 | loop fusion | flops 1834752 | bytes 3671040 | tf_op jit(solution)/shard_map/reduce_sum | solution.py:15
  159.3 0.6 copy-done.1
  159.9 0.6 multiply_reduce_fusion.1
  160.5 2.5 %copy.13 = bf16[256,3584]{0,1:T(8,128)(2,1)} copy(bf16[256,3584]{1,0:T(8,128)(2,1)S(1)} %get-tuple-element.19) | data formatting | bytes 3670016 | tf_op jit(solution)/shard_map/convert_element_type | solution.py:16
  162.9 0.0 copy-done.3
  162.9 3.8 %all-to-all-start = ((bf16[256,8,448]{0,2,1:T(8,128)(2,1)}), bf16[256,8,448]{0,2,1:T(8,128)(2,1)S(1)}, u32[]{:S(2)}, u32[]{:S(2)}) async-start(bf16[256,8,448]{0,2,1:T(8,128)(2,1)} %bitcast.12), calls=%async_computation | async-start | bytes 3670016 | tf_op jit(solution)/shard_map/all_to_all | solution.py:34
  166.7 0.0 copy-done.9
  166.7 26.9 %all-gather = s32[8,1,256]{2,1,0:T(1,128)S(1)} all-gather(s32[1,1,256]{2,1,0:T(1,128)S(1)} %bitcast.16), channel_id=1, replica_groups=mesh['dp'=8,'mp'=4] {'dp'}, dimensions={0}, use_global_device_ids=true | all-gather | bytes 9216 | tf_op jit(solution)/shard_map/all_gather | solution.py:33
  193.6 1.0 convert_reduce_fusion
  194.6 0.0 copy-start.8
  194.6 0.0 all-to-all-done
  194.6 0.0 copy-start.6
  194.6 0.2 copy.15
  194.8 1.3 copy-done.6
  196.1 3.8 %divide_convert_fusion = (bf16[1024,448]{0,1:T(8,128)(2,1)}, f32[1024,448]{0,1:T(8,128)}) fusion(f32[1024]{0:T(1024)S(1)} %multiply_add_fusion.1, bf16[2048,448]{0,1:T(8,128)(2,1)S(1)} %bitcast.13, s32[2048]{0:T(1024)S(1)} %bitcast.15, s32[1024]{0:T(1024)S(1)} %iota_add_fusion, f32[1024,448]{0,1:T(8,128)S(1)} %copy-done.6), kind=kOutput, calls=%fused_computation.10 | convolution fusion | flops 1883439104 | bytes 6438912 | tf_op jit(solution)/shard_map/while/body/eval_jaxpr/dot_general | solution.py:49
  199.9 0.0 copy-done.8
  199.9 4.7 %multiply_reduce_fusion = f32[1024]{0:T(1024)S(1)} fusion(bf16[1024,3584]{0,1:T(8,128)(2,1)} %all-gather.3.cloned.1.call-done), kind=kLoop, calls=%fused_computation | loop fusion | flops 11009024 | bytes 7344128 | tf_op jit(solution)/shard_map/reduce_sum | solution.py:25
  204.6 0.0 copy-done.4
  204.6 0.4 copy-done.2
  205.1 3.0 %fusion.6 = f32[256,1024]{1,0:T(8,128)} fusion(bf16[256,3584]{1,0:T(8,128)(2,1)S(1)} %copy-done.4, bf16[1024,3584]{0,1:T(8,128)(2,1)S(1)} %copy-done.2, f32[1024]{0:T(1024)S(1)} %multiply_reduce_fusion, f32[256]{0:T(256)S(1)} %get-tuple-element.18), kind=kOutput, calls=%fused_computation.14 | convolution fusion | flops 1879834624 | bytes 10228736 | tf_op jit(solution)/shard_map/dot_general | solution.py:21
  (10 shorter events, 0.0 us)
Async XLA Ops:
  8.0 1.0 copy-start
  8.0 148.7 %all-reduce.2.cloned.1.call-start = ((), (), s32[]{:S(2)}) async-start(), calls=%async_computation.1 | async-start | bytes 7340032 | tf_op jit(solution)/shard_map/psum | solution.py:14
  15.8 1.5 copy-start.5
  15.8 1.5 copy-start.7
  15.8 184.1 %all-gather.3.cloned.1.call-start = ((), (), s32[]{:S(2)}) async-start(), calls=%async_computation.2 | async-start | bytes 8257536 | tf_op jit(solution)/shard_map/all_gather | solution.py:20
  156.7 3.1 %copy-start.1 = (f32[256,3584]{1,0:T(8,128)S(1)}, f32[256,3584]{1,0:T(8,128)}, u32[]{:S(2)}) copy-start(f32[256,3584]{1,0:T(8,128)} %all-reduce.2.cloned.1.call-done) | copy-start | bytes 11010052
  160.5 2.5 %copy-start.3 = (bf16[256,3584]{1,0:T(8,128)(2,1)}, bf16[256,3584]{1,0:T(8,128)(2,1)S(1)}, u32[]{:S(2)}) copy-start(bf16[256,3584]{1,0:T(8,128)(2,1)S(1)} %get-tuple-element.19) | copy-start | bytes 5505028
  162.9 3.8 %copy-start.9 = (s32[256]{0:T(256)S(1)}, s32[256]{0:T(256)}, u32[]{:S(2)}) copy-start(s32[256]{0:T(256)} %param.7) | copy-start | bytes 3076
  162.9 31.6 %all-to-all-start = ((bf16[256,8,448]{0,2,1:T(8,128)(2,1)}), bf16[256,8,448]{0,2,1:T(8,128)(2,1)S(1)}, u32[]{:S(2)}, u32[]{:S(2)}) async-start(bf16[256,8,448]{0,2,1:T(8,128)(2,1)} %bitcast.12), calls=%async_computation | async-start | bytes 3670016 | tf_op jit(solution)/shard_map/all_to_all | solution.py:34
  194.6 5.3 %copy-start.8 = (f32[1024]{0:T(1024)}, f32[1024]{0:T(1024)S(1)}, u32[]{:S(2)}) copy-start(f32[1024]{0:T(1024)S(1)} %multiply_add_fusion.1) | copy-start | bytes 12292
  194.6 1.5 copy-start.6
  196.1 8.5 %copy-start.4 = (bf16[256,3584]{1,0:T(8,128)(2,1)S(1)}, bf16[256,3584]{1,0:T(8,128)(2,1)}, u32[]{:S(2)}) copy-start(bf16[256,3584]{1,0:T(8,128)(2,1)} %copy-done.3) | copy-start | bytes 5505028
  199.9 5.2 %copy-start.2 = (bf16[1024,3584]{0,1:T(8,128)(2,1)S(1)}, bf16[1024,3584]{0,1:T(8,128)(2,1)}, u32[]{:S(2)}) copy-start(bf16[1024,3584]{0,1:T(8,128)(2,1)} %all-gather.3.cloned.1.call-done) | copy-start | bytes 22020100
Sparse Core Ops, SparseCore 0:
  16.0 140.7 all-reduce.1
Sparse Core Ops, SparseCore 1:
  18.8 52.4 all-gather.2
where the time goes:
time: 216 us
  waiting for transfers between devices  138 us (64%)
  blocking collectives  26.9 us (12%)
  between operations  15.5 us (7%)
  matrix products  13.6 us (6%)
  other arithmetic  9.94 us (5%)
  local copies, waits for them, and re-layouts  7.42 us (3%)
  starting transfers between devices  3.87 us (2%)
    psum x1, waiting for transfers between devices, body(): projected = lax.psum(partial_value, 'mp')  138 us
    all_gather x1, blocking collectives, body(): every_assign = lax.all_gather(assignments, 'dp', axis=0, tiled=True)  26.9 us
    dot_general x1, matrix products, body(): partial_value = jnp.dot(pooled, w_out, preferred_element_type=jnp.float32)  6.79 us
    reduce_sum x1, other arithmetic, body(): center_norms = jnp.sum(piece_wide * piece_wide, axis=1)  4.74 us
    unnamed x20, local copies, waits for them, and re-layouts  4.72 us
  transfers between devices with their start and end apart: 3, of which 1 were waited for; matrix products, arithmetic and copies ran while one was open for 5% of the time, Pallas kernels for 0%

commit v1 on v0

v1 whole, which is shorter than its diff:
```python
import functools
import math

import jax
import jax.numpy as jnp
from jax import lax
from jax.experimental import pallas as pl
from jax.experimental.pallas import tpu as pltpu
from jax.sharding import PartitionSpec as P

EPSILON = 1e-06
EMA_DECAY = 0.9
BF = jnp.bfloat16
F32 = jnp.float32
ORDER = (0, 2, 1, 3)


def plain_body(pooled, w_out, assignments, ema_sums, ema_counts):
    partial_value = jnp.dot(pooled, w_out, preferred_element_type=F32)
    projected = lax.psum(partial_value, "mp")
    inverse_norm = 1.0 / jnp.sqrt(jnp.sum(projected * projected, axis=1, keepdims=True) + EPSILON)
    embedded = (projected * inverse_norm).astype(BF)
    local_centers = ema_sums.shape[0]
    doc_rows = embedded.shape[0]
    centers = (ema_sums / ema_counts[:, None]).astype(BF)
    column_piece = lax.all_gather(centers, "dp", axis=1, tiled=True)
    products = lax.dot_general(
        embedded, column_piece, (((1,), (1,)), ((), ())), preferred_element_type=F32
    )
    piece_wide = column_piece.astype(F32)
    center_norms = jnp.sum(piece_wide * piece_wide, axis=1)
    embed_wide = embedded.astype(F32)
    doc_norms = jnp.sum(embed_wide * embed_wide, axis=1)
    distances = doc_norms[:, None] + center_norms[None, :] - 2.0 * products
    first_center = lax.axis_index("mp") * local_centers
    center_ids = first_center + jnp.arange(local_centers, dtype=jnp.int32)
    feature_cols = ema_sums.shape[1]
    every_assign = lax.all_gather(assignments, "dp", axis=0, tiled=True)
    own_columns = lax.all_to_all(embedded, "dp", split_axis=1, concat_axis=0, tiled=True)
    shard_count = lax.axis_size("dp")
    group_size = math.gcd(shard_count, max(1, 2048 // doc_rows))
    block_rows = group_size * doc_rows
    turns = shard_count // group_size

    def add_block(block_index, totals):
        sums_now, counts_now = totals
        block_assign = lax.dynamic_slice_in_dim(every_assign, block_index * block_rows, block_rows, 0)
        block_columns = lax.dynamic_slice_in_dim(own_columns, block_index * block_rows, block_rows, 0)
        one_hot = (block_assign[None, :] == center_ids[:, None]).astype(BF)
        sums_now = sums_now + jnp.dot(one_hot, block_columns, preferred_element_type=F32)
        counts_now = counts_now + jnp.sum(one_hot, axis=1, dtype=F32)
        return (sums_now, counts_now)

    start_sums = (jnp.zeros((local_centers, feature_cols), F32), jnp.zeros((local_centers,), F32))
    batch_sums, batch_counts = lax.fori_loop(0, turns, add_block, start_sums)
    return finish(distances, batch_sums, batch_counts, ema_sums, ema_counts)


def finish(distances, batch_sums, batch_counts, ema_sums, ema_counts):
    new_counts = EMA_DECAY * ema_counts + (1.0 - EMA_DECAY) * batch_counts
    new_sums = EMA_DECAY * ema_sums + (1.0 - EMA_DECAY) * batch_sums
    new_centroids = (new_sums / new_counts[:, None]).astype(BF)
    return (distances, new_sums, new_counts, new_centroids)


def kernel(
    pooled_ref, w_hbm, cent_own, asg_own,
    dist_ref, sums_ref, counts_ref,
    w_ref, pf, send_far, send_near, relay, finals, embf, own, cent, asg, onehot,
    w_sem, cs, cr, as_, ar, zs, zr, fs, fr, gs, gr, es, er,
):
    d = lax.axis_index("dp")
    m = lax.axis_index("mp")
    docs = pooled_ref.shape[0]
    quarter = docs // 4
    dim = w_ref.shape[1]
    chunk = dim // 4
    feats, centers = cent_own.shape
    half = feats // 2
    core, xi, yi = d % 2, (d // 2) % 2, d // 4

    def partner(k):
        return ((yi + k // 4) % 2) * 4 + ((xi + (k // 2) % 2) % 2) * 2 + (core + k % 2) % 2

    right, left, far = (m + 1) % 4, (m + 3) % 4, (m + 2) % 4
    PC, XN, YN, DG = partner(1), partner(2), partner(4), partner(6)

    def remote(src, dst, ssem, rsem, dp, mp):
        return pltpu.make_async_remote_copy(
            src_ref=src, dst_ref=dst, send_sem=ssem, recv_sem=rsem,
            device_id={"dp": dp, "mp": mp}, device_id_type=pl.DeviceIdType.MESH,
        )

    def cols(c):
        return pl.ds(c * chunk, chunk)

    def rows(q):
        return pl.ds(pl.multiple_of(q * quarter, quarter), quarter)

    w_copies = {}
    for c in ORDER:
        w_copies[c] = pltpu.make_async_copy(w_hbm.at[:, cols(c)], w_ref.at[:, cols(c)], w_sem.at[c])
        w_copies[c].start()

    barrier = pltpu.get_barrier_semaphore()
    for k in range(1, 8):
        pl.semaphore_signal(barrier, inc=1, device_id={"dp": partner(k), "mp": m}, device_id_type=pl.DeviceIdType.MESH)
    for z in (right, left):
        pl.semaphore_signal(barrier, inc=1, device_id={"dp": d, "mp": z}, device_id_type=pl.DeviceIdType.MESH)
    pl.semaphore_wait(barrier, 9)

    def slot(b):
        return cent.at[pl.ds(pl.multiple_of(b * feats, feats), feats), :]

    def half_slot(b, h):
        return cent.at[pl.ds(pl.multiple_of(b * feats + h * half, half), half), :]

    sends = []

    def go(copy):
        copy.start()
        sends.append(copy)
        return copy

    asg_copies = {}
    for k in range(1, 8):
        asg_copies[k] = go(remote(asg_own, asg.at[d], as_.at[k], ar.at[k], partner(k), m))
    c_x = go(remote(cent_own, slot(d), cs.at[0], cr.at[0], XN, m))
    c_y = go(remote(cent_own, slot(d), cs.at[1], cr.at[1], YN, m))
    c_p = go(remote(cent_own, slot(d), cs.at[2], cr.at[2], PC, m))

    z_copies = {}
    for c in ORDER:
        w_copies[c].wait()
        pf[:, cols(c)] = jnp.dot(pooled_ref[...], w_ref[:, cols(c)], preferred_element_type=F32)
        send_far[:, cols(c)] = pf[rows(far), cols(c)].astype(BF)
        z_copies[c] = go(remote(
            send_far.at[:, cols(c)], relay.at[:, cols(c)], zs.at[c], zr.at[c], d, right if c < 2 else left))
        side = 1 if c < 2 else 0
        to = left if c < 2 else right
        send_near[side, :, cols(c)] = pf[rows(to), cols(c)].astype(BF)
        z_copies[(side, c)] = go(remote(
            send_near.at[side, :, cols(c)], finals.at[side, :, cols(c)], fs.at[side, c], fr.at[side, c], d, to))
    for c in ORDER:
        z_copies[c].wait_recv()
        side = 0 if c < 2 else 1
        to = right if c < 2 else left
        send_near[side, :, cols(c)] = (pf[rows(to), cols(c)] + relay[:, cols(c)].astype(F32)).astype(BF)
        z_copies[(side, c)] = go(remote(
            send_near.at[side, :, cols(c)], finals.at[side, :, cols(c)], fs.at[side, c], fr.at[side, c], d, to))

    first_center = m * centers
    ids = first_center + lax.broadcasted_iota(jnp.int32, (centers, docs), 0)
    counts = jnp.zeros((8, centers), F32)
    for k in range(8):
        if k:
            asg_copies[k].wait_recv()
            row = asg[partner(k)][0:1, :]
        else:
            row = asg_own[0:1, :]
        onehot[k] = jnp.where(ids == row, 1.0, 0.0).astype(BF)
        counts = counts + lax.dot_general(
            jnp.ones((8, docs), BF), onehot[k], (((1,), (1,)), ((), ())), preferred_element_type=F32)
    counts_ref[...] = counts

    total = jnp.zeros((quarter, 1), F32)
    for c in ORDER:
        for side in (0, 1):
            z_copies[(side, c)].wait_recv()
        part = pf[rows(m), cols(c)] + finals[0, :, cols(c)].astype(F32) + finals[1, :, cols(c)].astype(F32)
        pf[rows(m), cols(c)] = part
        total = total + jnp.sum(part * part, axis=1, keepdims=True)
    inverse = 1.0 / jnp.sqrt(total + EPSILON)
    mine = pf[rows(m), :] * inverse
    for b in range(8):
        embf[b, rows(m), :] = mine[:, b * feats:(b + 1) * feats].astype(BF)

    def emb(q, lo):
        return embf.at[pl.ds(lo, 4), rows(q), :]

    g_copies = {}
    for step in (0, 1):
        for side, to in ((0, right), (1, left)):
            lo = 4 * ((step + side) % 2)
            g_copies[(side, step)] = go(remote(emb(m, lo), emb(m, lo), gs.at[side, step], gr.at[side, step], d, to))

    e_copies = {}

    def scatter(r):
        q = (m + r) % 4
        for k in (1, 2, 4, 6, 3, 5, 7):
            e_copies[(r, k)] = go(remote(
                embf.at[partner(k), rows(q), :], own.at[d, rows(q), :], es.at[r, k], er.at[r, k], partner(k), m))

    c_x.wait_recv()
    c_rx = go(remote(half_slot(XN, 0), half_slot(XN, 0), cs.at[3], cr.at[3], YN, m))
    c_px = go(remote(slot(XN), slot(XN), cs.at[5], cr.at[5], PC, m))
    c_y.wait_recv()
    c_ry = go(remote(half_slot(YN, 1), half_slot(YN, 1), cs.at[4], cr.at[4], XN, m))
    c_py = go(remote(slot(YN), slot(YN), cs.at[6], cr.at[6], PC, m))
    scatter(0)

    g_copies[(0, 0)].wait_recv()
    g_copies[(0, 2)] = go(remote(emb(left, 0), emb(left, 0), gs.at[0, 2], gr.at[0, 2], d, right))
    g_copies[(1, 0)].wait_recv()
    g_copies[(1, 2)] = go(remote(emb(right, 4), emb(right, 4), gs.at[1, 2], gr.at[1, 2], d, left))
    g_copies[(0, 1)].wait_recv()
    scatter(3)
    g_copies[(1, 1)].wait_recv()
    scatter(1)
    c_rx.wait_recv()
    c_pd0 = go(remote(half_slot(DG, 0), half_slot(DG, 0), cs.at[7], cr.at[7], PC, m))
    c_ry.wait_recv()
    c_pd1 = go(remote(half_slot(DG, 1), half_slot(DG, 1), cs.at[8], cr.at[8], PC, m))
    g_copies[(0, 2)].wait_recv()
    g_copies[(1, 2)].wait_recv()
    scatter(2)

    doc_norms = jnp.zeros((docs, 1), F32)
    for b in range(8):
        wide = embf[b].astype(F32)
        doc_norms = doc_norms + jnp.sum(wide * wide, axis=1, keepdims=True)
    norms = jnp.zeros((1, centers), F32)
    waits = {1: (c_p,), 3: (c_px,), 5: (c_py,), 7: (c_pd0, c_pd1)}
    for k in (0, 2, 4, 6, 1, 3, 5, 7):
        for copy in waits.get(k, ()):
            copy.wait_recv()
        block = slot(partner(k))[...] if k else cent_own[...]
        wide = block.astype(F32)
        norms = norms + jnp.sum(wide * wide, axis=0, keepdims=True)
        product = jnp.dot(embf[partner(k)], block, preferred_element_type=F32)
        if k == 0:
            dist_ref[...] = product
        elif k < 7:
            dist_ref[...] += product
        else:
            dist_ref[...] = doc_norms + norms - 2.0 * (dist_ref[...] + product)

    sums_ref[...] = jnp.dot(onehot[0], embf[d], preferred_element_type=F32)
    for k in (1, 2, 4, 6, 3, 5, 7):
        for r in range(4):
            e_copies[(r, k)].wait_recv()
        sums_ref[...] += jnp.dot(onehot[k], own[partner(k)], preferred_element_type=F32)
    for copy in sends:
        copy.wait_send()


def fast_body(pooled, w_out, assignments, ema_sums, ema_counts):
    docs, depth = pooled.shape
    dim = w_out.shape[1]
    centers, feats = ema_sums.shape
    quarter = docs // 4
    cent = (ema_sums / ema_counts[:, None]).astype(BF).T
    asg8 = jnp.broadcast_to(assignments[None, :], (8, docs))
    vmem = pl.BlockSpec(memory_space=pltpu.VMEM)
    dma = pltpu.SemaphoreType.DMA
    distances, batch_sums, counts = pl.pallas_call(
        kernel,
        out_shape=(
            jax.ShapeDtypeStruct((docs, centers), F32),
            jax.ShapeDtypeStruct((centers, feats), F32),
            jax.ShapeDtypeStruct((8, centers), F32),
        ),
        in_specs=[vmem, pl.BlockSpec(memory_space=pl.ANY), vmem, vmem],
        out_specs=(vmem, vmem, vmem),
        scratch_shapes=[
            pltpu.VMEM((depth, dim), BF),
            pltpu.VMEM((docs, dim), F32),
            pltpu.VMEM((quarter, dim), BF),
            pltpu.VMEM((2, quarter, dim), BF),
            pltpu.VMEM((quarter, dim), BF),
            pltpu.VMEM((2, quarter, dim), BF),
            pltpu.VMEM((8, docs, feats), BF),
            pltpu.VMEM((8, docs, feats), BF),
            pltpu.VMEM((8 * feats, centers), BF),
            pltpu.VMEM((8, 8, docs), jnp.int32),
            pltpu.VMEM((8, centers, docs), BF),
            dma((4,)), dma((9,)), dma((9,)), dma((8,)), dma((8,)), dma((4,)), dma((4,)),
            dma((2, 4)), dma((2, 4)), dma((2, 3)), dma((2, 3)), dma((4, 8)), dma((4, 8)),
        ],
        compiler_params=pltpu.CompilerParams(
            collective_id=0, has_side_effects=True, vmem_limit_bytes=60 * 1024 * 1024),
        name="embed_and_assign",
    )(pooled, w_out, cent, asg8)
    return finish(distances, batch_sums, counts[0], ema_sums, ema_counts)


def solution(mesh):
    fast = mesh.shape["dp"] == 8 and mesh.shape["mp"] == 4
    return jax.shard_map(
        fast_body if fast else plain_body,
        mesh=mesh,
        in_specs=(P("dp", "mp"), P("mp", None), P("dp"), P("mp", "dp"), P("mp")),
        out_specs=(P("dp", "mp"), P("mp", "dp"), P("mp"), P("mp", "dp")),
        check_vma=False,
    )
```

time: 216 us -> 96.6 us (0.45)
  waiting for transfers between devices: 138 us -> 0 us
  Pallas kernels: 0 us -> 83.2 us
  blocking collectives: 26.9 us -> 0 us
  between operations: 15.5 us -> 0.68 us
  matrix products: 13.6 us -> 0 us
  other arithmetic: 9.94 us -> 6.01 us
  starting transfers between devices: 3.87 us -> 0 us
    psum x1 -> x0, waiting for transfers between devices: 138 us -> none  [body(): projected = lax.psum(partial_value, 'mp')]
    pallas_call x0 -> x1, Pallas kernels: none -> 83.2 us  [fast_body(): pl.pallas_call(kernel, out_shape=(jax.ShapeDtypeStruct((docs, centers), F...]
    all_gather x1 -> x0, blocking collectives: 26.9 us -> none  [body(): every_assign = lax.all_gather(assignments, 'dp', axis=0, tiled=True)]
    dot_general x3 -> x0, matrix products: 13.6 us -> none  [the longest x1 6.79 us: body(): partial_value = jnp.dot(pooled, w_out, preferred_element_type=jnp.float32)]
    reduce_sum x4 -> x0, other arithmetic: 8.77 us -> none  [the longest x1 4.74 us: body(): center_norms = jnp.sum(piece_wide * piece_wide, axis=1)]
    all_to_all x1 -> x0, starting transfers between devices: 3.79 us -> none  [body(): lax.all_to_all(embedded, 'dp', split_axis=1, concat_axis=0, tiled=True)]
    transpose x0 -> x1, other arithmetic: none -> 2.64 us  [fast_body(): cent = (ema_sums / ema_counts[:, None]).astype(BF).T]
    convert_element_type x1 -> x0, local copies, waits for them, and re-layouts: 2.47 us -> none  [body(): embedded = (projected * inverse_norm).astype(jnp.bfloat16)]
  transfers between devices with their start and end apart: 3 -> 0, of which waited for: 1 -> 0; matrix products, arithmetic and copies ran while one was open for 5% -> 0% of each run, Pallas kernels for 0% -> 0%
where the time goes in v1:
time: 96.6 us; the launch traced here: 96.3 us
  Pallas kernels  83.2 us (86%)
  local copies, waits for them, and re-layouts  6.41 us (7%)
  other arithmetic  6.01 us (6%)
    pallas_call x1, Pallas kernels, fast_body(): pl.pallas_call(kernel, out_shape=(jax.ShapeDtypeStruct((docs, centers), F...  83.2 us
    unnamed x14, local copies, waits for them, and re-layouts  5.81 us
    transpose x1, other arithmetic, fast_body(): cent = (ema_sums / ema_counts[:, None]).astype(BF).T  2.64 us
    convert_element_type x1, other arithmetic, finish(): new_centroids = (new_sums / new_counts[:, None]).astype(BF)  2.6 us

profile of v1, /device:TPU:0, one launch (start us, length us, event | category | flops | bytes accessed | tf_op | source)
XLA Modules:
  0.0 96.3 jit_solution(6436559259888631508)
XLA Ops:
  0.6 0.0 copy-start.4
  0.6 2.6 %fusion.cent_own = bf16[448,1024]{1,0:T(8,128)(2,1)} fusion(f32[1024,448]{0,1:T(8,128)} %param.8, f32[1024]{0:T(1024)} %param.9), kind=kLoop, calls=%fused_computation.3 | loop fusion | flops 917504 | bytes 2756608 | tf_op jit(solution)/shard_map/transpose | solution.py:253
  3.3 0.0 copy-done.4
  3.3 0.6 broadcast_in_dim.2.asg_own
  3.9 0.0 copy-start.2
  3.9 0.0 copy-start
  3.9 83.2 %embed_and_assign.1 = (f32[256,1024]{1,0:T(8,128)}, f32[1024,448]{1,0:T(8,128)}, f32[8,1024]{1,0:T(8,128)}) custom-call(bf16[256,896]{1,0:T(8,128)(2,1)} %pooled_ref.1, bf16[896,3584]{1,0:T(8,128)(2,1)} %w_hbm.1, bf16[448,1024]{1,0:T(8,128)(2,1)} %fusion.cent_own, s32[8,256]{1,0:T(8,128)} %broadcast_in_dim.2.asg_own), custom_call_target="tpu_custom_call" | custom-call | tf_op jit(solution)/shard_map/embed_and_assign/pallas_call | solution.py:257
  87.1 0.8 slice_multiply_fusion
  87.9 0.0 copy-done.2
  87.9 0.0 copy-start.3
  87.9 0.0 copy-done
  87.9 1.8 %copy.9 = f32[1024,448]{1,0:T(8,128)} copy(f32[1024,448]{0,1:T(8,128)S(1)} %copy-done) | data formatting | bytes 3670016 | tf_op args[3]
  89.7 2.6 %divide_convert_fusion = (bf16[1024,448]{1,0:T(8,128)(2,1)S(1)}, f32[1024,448]{1,0:T(8,128)S(1)}) fusion(f32[1024]{0:T(1024)S(1)} %multiply_add_fusion.1, f32[1024,448]{1,0:T(8,128)} %get-tuple-element.8, f32[1024,448]{1,0:T(8,128)} %copy.9), kind=kLoop, calls=%fused_computation | loop fusion | flops 2293760 | bytes 6426624 | tf_op jit(solution)/shard_map/convert_element_type | solution.py:62
  92.3 0.0 copy-done.3
  92.3 1.7 %copy.10 = f32[1024,448]{0,1:T(8,128)} copy(f32[1024,448]{1,0:T(8,128)S(1)} %get-tuple-element.15) | data formatting | bytes 3670016
  94.1 0.0 copy-start.1
  94.1 1.3 %copy.11 = bf16[1024,448]{0,1:T(8,128)(2,1)} copy(bf16[1024,448]{1,0:T(8,128)(2,1)S(1)} %get-tuple-element.14) | data formatting | bytes 1835008
  95.3 0.0 copy-done.1
  95.3 1.0 %copy.13 = f32[256,1024]{1,0:T(8,128)} copy(f32[256,1024]{1,0:T(8,128)S(1)} %copy-done.1) | data formatting | bytes 2097152
  (1 shorter events, 0.0 us)
Async XLA Ops:
  0.6 2.7 %copy-start.4 = (s32[256]{0:T(256)S(1)}, s32[256]{0:T(256)}, u32[]{:S(2)}) copy-start(s32[256]{0:T(256)} %param.7) | copy-start | bytes 3076
  3.9 84.0 %copy-start.2 = (f32[1024]{0:T(1024)S(1)}, f32[1024]{0:T(1024)}, u32[]{:S(2)}) copy-start(f32[1024]{0:T(1024)} %param.9) | copy-start | bytes 12292
  3.9 84.0 %copy-start = (f32[1024,448]{0,1:T(8,128)S(1)}, f32[1024,448]{0,1:T(8,128)}, u32[]{:S(2)}) copy-start(f32[1024,448]{0,1:T(8,128)} %param.8) | copy-start | bytes 5505028
  87.9 4.4 %copy-start.3 = (f32[1024]{0:T(1024)}, f32[1024]{0:T(1024)S(1)}, u32[]{:S(2)}) copy-start(f32[1024]{0:T(1024)S(1)} %multiply_add_fusion.1) | copy-start | bytes 12292
  94.1 1.3 %copy-start.1 = (f32[256,1024]{1,0:T(8,128)S(1)}, f32[256,1024]{1,0:T(8,128)}, u32[]{:S(2)}) copy-start(f32[256,1024]{1,0:T(8,128)} %get-tuple-element.20) | copy-start | bytes 3145732

commit v2 on v1

--- a/solution.py
+++ b/solution.py
@@ -12,7 +12,6 @@
 EMA_DECAY = 0.9
 BF = jnp.bfloat16
 F32 = jnp.float32
-ORDER = (0, 2, 1, 3)
 
 
 def plain_body(pooled, w_out, assignments, ema_sums, ema_counts):
@@ -66,8 +65,8 @@
 def kernel(
     pooled_ref, w_hbm, cent_own, asg_own,
     dist_ref, sums_ref, counts_ref,
-    w_ref, pf, send_far, send_near, relay, finals, embf, own, cent, asg, onehot,
-    w_sem, cs, cr, as_, ar, zs, zr, fs, fr, gs, gr, es, er,
+    w_ref, pf, outgoing, incoming, embf, own, cent, asg, onehot,
+    w_sem, cs, cr, as_, ar, zs, zr, gs, gr, es, er,
 ):
     d = lax.axis_index("dp")
     m = lax.axis_index("mp")
@@ -82,7 +81,11 @@
     def partner(k):
         return ((yi + k // 4) % 2) * 4 + ((xi + (k // 2) % 2) % 2) * 2 + (core + k % 2) % 2
 
-    right, left, far = (m + 1) % 4, (m + 3) % 4, (m + 2) % 4
+    near = m // 2
+    far = 1 - near
+    inner = (m + near) % 2
+    ahead = m + 1 - 2 * near
+    behind = m - inner * (1 - 2 * near) + (1 - inner) * (1 - 2 * near)
     PC, XN, YN, DG = partner(1), partner(2), partner(4), partner(6)
 
     def remote(src, dst, ssem, rsem, dp, mp):
@@ -94,26 +97,33 @@
     def cols(c):
         return pl.ds(c * chunk, chunk)
 
-    def rows(q):
-        return pl.ds(pl.multiple_of(q * quarter, quarter), quarter)
-
-    w_copies = {}
-    for c in ORDER:
-        w_copies[c] = pltpu.make_async_copy(w_hbm.at[:, cols(c)], w_ref.at[:, cols(c)], w_sem.at[c])
+    def rows(flow, i):
+        return pl.ds(pl.multiple_of((flow * 2 + i) * quarter, quarter), quarter)
+
+    w_copies = []
+    for c in range(4):
+        w_copies.append(pltpu.make_async_copy(w_hbm.at[:, cols(c)], w_ref.at[:, cols(c)], w_sem.at[c]))
         w_copies[c].start()
 
     barrier = pltpu.get_barrier_semaphore()
     for k in range(1, 8):
         pl.semaphore_signal(barrier, inc=1, device_id={"dp": partner(k), "mp": m}, device_id_type=pl.DeviceIdType.MESH)
-    for z in (right, left):
-        pl.semaphore_signal(barrier, inc=1, device_id={"dp": d, "mp": z}, device_id_type=pl.DeviceIdType.MESH)
-    pl.semaphore_wait(barrier, 9)
+    pl.semaphore_signal(barrier, inc=1, device_id={"dp": d, "mp": ahead}, device_id_type=pl.DeviceIdType.MESH)
+
+    @pl.when(inner == 1)
+    def _():
+        pl.semaphore_signal(barrier, inc=1, device_id={"dp": d, "mp": behind}, device_id_type=pl.DeviceIdType.MESH)
+
+    pl.semaphore_wait(barrier, 8 + inner)
 
     def slot(b):
         return cent.at[pl.ds(pl.multiple_of(b * feats, feats), feats), :]
 
     def half_slot(b, h):
         return cent.at[pl.ds(pl.multiple_of(b * feats + h * half, half), half), :]
+
+    def half_own(h):
+        return cent_own.at[pl.ds(h * half, half), :]
 
     sends = []
 
@@ -122,32 +132,134 @@
         sends.append(copy)
         return copy
 
+    c_x, c_y = {}, {}
+    for h in (0, 1):
+        c_x[h] = go(remote(half_own(h), half_slot(d, h), cs.at[h], cr.at[h], XN, m))
+        g = 1 - h
+        c_y[g] = go(remote(half_own(g), half_slot(d, g), cs.at[2 + g], cr.at[2 + g], YN, m))
+    c_p = go(remote(cent_own, slot(d), cs.at[4], cr.at[4], PC, m))
     asg_copies = {}
     for k in range(1, 8):
         asg_copies[k] = go(remote(asg_own, asg.at[d], as_.at[k], ar.at[k], partner(k), m))
-    c_x = go(remote(cent_own, slot(d), cs.at[0], cr.at[0], XN, m))
-    c_y = go(remote(cent_own, slot(d), cs.at[1], cr.at[1], YN, m))
-    c_p = go(remote(cent_own, slot(d), cs.at[2], cr.at[2], PC, m))
-
-    z_copies = {}
-    for c in ORDER:
+
+    def sum_copy(flow, i, c, to):
+        at = (flow, pl.ds(i * quarter, quarter), cols(c))
+        return remote(outgoing.at[at], incoming.at[at], zs.at[flow, i, c], zr.at[flow, i, c], d, to)
+
+    def put(flow, i, c, value):
+        outgoing[flow, pl.ds(i * quarter, quarter), cols(c)] = value.astype(BF)
+
+    def arrived(flow, i, c):
+        return pf[rows(flow, i), cols(c)] + incoming[flow, pl.ds(i * quarter, quarter), cols(c)].astype(F32)
+
+    for c in range(4):
         w_copies[c].wait()
         pf[:, cols(c)] = jnp.dot(pooled_ref[...], w_ref[:, cols(c)], preferred_element_type=F32)
-        send_far[:, cols(c)] = pf[rows(far), cols(c)].astype(BF)
-        z_copies[c] = go(remote(
-            send_far.at[:, cols(c)], relay.at[:, cols(c)], zs.at[c], zr.at[c], d, right if c < 2 else left))
-        side = 1 if c < 2 else 0
-        to = left if c < 2 else right
-        send_near[side, :, cols(c)] = pf[rows(to), cols(c)].astype(BF)
-        z_copies[(side, c)] = go(remote(
-            send_near.at[side, :, cols(c)], finals.at[side, :, cols(c)], fs.at[side, c], fr.at[side, c], d, to))
-    for c in ORDER:
-        z_copies[c].wait_recv()
-        side = 0 if c < 2 else 1
-        to = right if c < 2 else left
-        send_near[side, :, cols(c)] = (pf[rows(to), cols(c)] + relay[:, cols(c)].astype(F32)).astype(BF)
-        z_copies[(side, c)] = go(remote(
-            send_near.at[side, :, cols(c)], finals.at[side, :, cols(c)], fs.at[side, c], fr.at[side, c], d, to))
+
+        @pl.when(inner == 0)
+        def _():
+            put(near, 0, c, pf[rows(near, 0), cols(c)])
+            sum_copy(near, 0, c, ahead).start()
+
+    @pl.when(inner == 0)
+    def _():
+        for c in range(4):
+            put(near, 1, c, pf[rows(near, 1), cols(c)])
+            sum_copy(near, 1, c, ahead).start()
+
+    def sum_near(i, c):
+        @pl.when(inner == 1)
+        def _():
+            sum_copy(near, i, c, ahead).wait_recv()
+            put(near, i, c, arrived(near, i, c))
+            sum_copy(near, i, c, ahead).start()
+
+    def sum_far(i, c):
+        sum_copy(far, i, c, behind).wait_recv()
+
+        @pl.when(inner == 1)
+        def _():
+            put(far, i, c, arrived(far, i, c))
+            sum_copy(far, i, c, behind).start()
+
+        @pl.when(inner == 0)
+        def _():
+            pf[rows(far, i), cols(c)] = arrived(far, i, c)
+
+    def emb_copy(flow, i, b, to):
+        ref = embf.at[pl.ds(2 * b, 2), rows(flow, i), :]
+        return remote(ref, ref, gs.at[flow, i, b], gr.at[flow, i, b], d, to)
+
+    def embed(i):
+        @pl.when(inner == 0)
+        def _():
+            value = pf[rows(far, i), :]
+            inverse = 1.0 / jnp.sqrt(jnp.sum(value * value, axis=1, keepdims=True) + EPSILON)
+            value = value * inverse
+            for b in range(8):
+                embf[b, rows(far, i), :] = value[:, b * feats:(b + 1) * feats].astype(BF)
+            for b in range(4):
+                emb_copy(far, i, b, ahead).start()
+
+    def emb_near(i, b):
+        @pl.when(inner == 1)
+        def _():
+            emb_copy(far, i, b, ahead).wait_recv()
+            emb_copy(far, i, b, ahead).start()
+
+    def emb_far(i, b):
+        emb_copy(near, i, b, behind).wait_recv()
+
+        @pl.when(inner == 1)
+        def _():
+            emb_copy(near, i, b, behind).start()
+
+    e_copies = {}
+
+    def scatter(name, flow, i):
+        for k in (1, 2, 4, 6, 3, 5, 7):
+            e_copies[(name, i, k)] = go(remote(
+                embf.at[partner(k), rows(flow, i), :], own.at[d, rows(flow, i), :],
+                es.at[flow, i, k], er.at[flow, i, k], partner(k), m))
+
+    for t in range(5):
+        if t < 4:
+            sum_near(0, t)
+        if t >= 1:
+            sum_far(0, t - 1)
+    embed(0)
+    c_x[0].wait_recv()
+    c_rx = go(remote(half_slot(XN, 0), half_slot(XN, 0), cs.at[5], cr.at[5], YN, m))
+    c_y[1].wait_recv()
+    c_ry = go(remote(half_slot(YN, 1), half_slot(YN, 1), cs.at[6], cr.at[6], XN, m))
+    for t in range(7):
+        if t < 4:
+            sum_near(1, t)
+        if 1 <= t < 5:
+            sum_far(1, t - 1)
+        if t == 4:
+            embed(1)
+        if 2 <= t < 6:
+            emb_near(0, t - 2)
+        if 3 <= t:
+            emb_far(0, t - 3)
+    scatter("far", far, 0)
+    scatter("near", near, 0)
+    c_x[1].wait_recv()
+    c_px = go(remote(slot(XN), slot(XN), cs.at[7], cr.at[7], PC, m))
+    c_y[0].wait_recv()
+    c_py = go(remote(slot(YN), slot(YN), cs.at[8], cr.at[8], PC, m))
+    for t in range(5):
+        if t < 4:
+            emb_near(1, t)
+        if t >= 1:
+            emb_far(1, t - 1)
+    scatter("far", far, 1)
+    scatter("near", near, 1)
+    c_rx.wait_recv()
+    c_pd0 = go(remote(half_slot(DG, 0), half_slot(DG, 0), cs.at[9], cr.at[9], PC, m))
+    c_ry.wait_recv()
+    c_pd1 = go(remote(half_slot(DG, 1), half_slot(DG, 1), cs.at[10], cr.at[10], PC, m))
 
     first_center = m * centers
     ids = first_center + lax.broadcasted_iota(jnp.int32, (centers, docs), 0)
@@ -162,59 +274,6 @@
         counts = counts + lax.dot_general(
             jnp.ones((8, docs), BF), onehot[k], (((1,), (1,)), ((), ())), preferred_element_type=F32)
     counts_ref[...] = counts
-
-    total = jnp.zeros((quarter, 1), F32)
-    for c in ORDER:
-        for side in (0, 1):
-            z_copies[(side, c)].wait_recv()
-        part = pf[rows(m), cols(c)] + finals[0, :, cols(c)].astype(F32) + finals[1, :, cols(c)].astype(F32)
-        pf[rows(m), cols(c)] = part
-        total = total + jnp.sum(part * part, axis=1, keepdims=True)
-    inverse = 1.0 / jnp.sqrt(total + EPSILON)
-    mine = pf[rows(m), :] * inverse
-    for b in range(8):
-        embf[b, rows(m), :] = mine[:, b * feats:(b + 1) * feats].astype(BF)
-
-    def emb(q, lo):
-        return embf.at[pl.ds(lo, 4), rows(q), :]
-
-    g_copies = {}
-    for step in (0, 1):
-        for side, to in ((0, right), (1, left)):
-            lo = 4 * ((step + side) % 2)
-            g_copies[(side, step)] = go(remote(emb(m, lo), emb(m, lo), gs.at[side, step], gr.at[side, step], d, to))
-
-    e_copies = {}
-
-    def scatter(r):
-        q = (m + r) % 4
-        for k in (1, 2, 4, 6, 3, 5, 7):
-            e_copies[(r, k)] = go(remote(
-                embf.at[partner(k), rows(q), :], own.at[d, rows(q), :], es.at[r, k], er.at[r, k], partner(k), m))
-
-    c_x.wait_recv()
-    c_rx = go(remote(half_slot(XN, 0), half_slot(XN, 0), cs.at[3], cr.at[3], YN, m))
-    c_px = go(remote(slot(XN), slot(XN), cs.at[5], cr.at[5], PC, m))
-    c_y.wait_recv()
-    c_ry = go(remote(half_slot(YN, 1), half_slot(YN, 1), cs.at[4], cr.at[4], XN, m))
-    c_py = go(remote(slot(YN), slot(YN), cs.at[6], cr.at[6], PC, m))
-    scatter(0)
-
-    g_copies[(0, 0)].wait_recv()
-    g_copies[(0, 2)] = go(remote(emb(left, 0), emb(left, 0), gs.at[0, 2], gr.at[0, 2], d, right))
-    g_copies[(1, 0)].wait_recv()
-    g_copies[(1, 2)] = go(remote(emb(right, 4), emb(right, 4), gs.at[1, 2], gr.at[1, 2], d, left))
-    g_copies[(0, 1)].wait_recv()
-    scatter(3)
-    g_copies[(1, 1)].wait_recv()
-    scatter(1)
-    c_rx.wait_recv()
-    c_pd0 = go(remote(half_slot(DG, 0), half_slot(DG, 0), cs.at[7], cr.at[7], PC, m))
-    c_ry.wait_recv()
-    c_pd1 = go(remote(half_slot(DG, 1), half_slot(DG, 1), cs.at[8], cr.at[8], PC, m))
-    g_copies[(0, 2)].wait_recv()
-    g_copies[(1, 2)].wait_recv()
-    scatter(2)
 
     doc_norms = jnp.zeros((docs, 1), F32)
     for b in range(8):
@@ -238,18 +297,29 @@
 
     sums_ref[...] = jnp.dot(onehot[0], embf[d], preferred_element_type=F32)
     for k in (1, 2, 4, 6, 3, 5, 7):
-        for r in range(4):
-            e_copies[(r, k)].wait_recv()
+        for i in range(2):
+            for name in ("far", "near"):
+                e_copies[(name, i, k)].wait_recv()
         sums_ref[...] += jnp.dot(onehot[k], own[partner(k)], preferred_element_type=F32)
     for copy in sends:
         copy.wait_send()
+    for i in range(2):
+        for c in range(4):
+            sum_copy(near, i, c, ahead).wait_send()
+            emb_copy(far, i, c, ahead).wait_send()
+
+    @pl.when(inner == 1)
+    def _():
+        for i in range(2):
+            for c in range(4):
+                sum_copy(far, i, c, behind).wait_send()
+                emb_copy(near, i, c, behind).wait_send()
 
 
 def fast_body(pooled, w_out, assignments, ema_sums, ema_counts):
     docs, depth = pooled.shape
     dim = w_out.shape[1]
     centers, feats = ema_sums.shape
-    quarter = docs // 4
     cent = (ema_sums / ema_counts[:, None]).astype(BF).T
     asg8 = jnp.broadcast_to(assignments[None, :], (8, docs))
     vmem = pl.BlockSpec(memory_space=pltpu.VMEM)
@@ -266,17 +336,15 @@
         scratch_shapes=[
             pltpu.VMEM((depth, dim), BF),
             pltpu.VMEM((docs, dim), F32),
-            pltpu.VMEM((quarter, dim), BF),
-            pltpu.VMEM((2, quarter, dim), BF),
-            pltpu.VMEM((quarter, dim), BF),
-            pltpu.VMEM((2, quarter, dim), BF),
+            pltpu.VMEM((2, docs // 2, dim), BF),
+            pltpu.VMEM((2, docs // 2, dim), BF),
             pltpu.VMEM((8, docs, feats), BF),
             pltpu.VMEM((8, docs, feats), BF),
             pltpu.VMEM((8 * feats, centers), BF),
             pltpu.VMEM((8, 8, docs), jnp.int32),
             pltpu.VMEM((8, centers, docs), BF),
-            dma((4,)), dma((9,)), dma((9,)), dma((8,)), dma((8,)), dma((4,)), dma((4,)),
-            dma((2, 4)), dma((2, 4)), dma((2, 3)), dma((2, 3)), dma((4, 8)), dma((4, 8)),
+            dma((4,)), dma((11,)), dma((11,)), dma((8,)), dma((8,)), dma((2, 2, 4)), dma((2, 2, 4)),
+            dma((2, 2, 4)), dma((2, 2, 4)), dma((2, 2, 8)), dma((2, 2, 8)),
         ],
         compiler_params=pltpu.CompilerParams(
             collective_id=0, has_side_effects=True, vmem_limit_bytes=60 * 1024 * 1024),

time: 96.6 us -> 93.5 us (0.968)
  Pallas kernels: 83.2 us -> 80.1 us
    pallas_call x1, Pallas kernels: 83.2 us -> 80.1 us  [fast_body(): pl.pallas_call(kernel, out_shape=(jax.ShapeDtypeStruct((docs, centers), F...]
where the time goes in v2:
time: 93.5 us; the launch traced here: 93.2 us
  Pallas kernels  80.1 us (86%)
  local copies, waits for them, and re-layouts  6.41 us (7%)
  other arithmetic  6.01 us (6%)
    pallas_call x1, Pallas kernels, fast_body(): pl.pallas_call(kernel, out_shape=(jax.ShapeDtypeStruct((docs, centers), F...  80.1 us
    unnamed x14, local copies, waits for them, and re-layouts  5.81 us
    transpose x1, other arithmetic, fast_body(): cent = (ema_sums / ema_counts[:, None]).astype(BF).T  2.64 us
    convert_element_type x1, other arithmetic, finish(): new_centroids = (new_sums / new_counts[:, None]).astype(BF)  2.6 us

profile of v2, /device:TPU:0, one launch (start us, length us, event | category | flops | bytes accessed | tf_op | source)
XLA Modules:
  0.0 93.2 jit_solution(6009255112532564926)
XLA Ops:
  0.6 0.0 copy-start.4
  0.6 2.6 %fusion.cent_own = bf16[448,1024]{1,0:T(8,128)(2,1)} fusion(f32[1024,448]{0,1:T(8,128)} %param.8, f32[1024]{0:T(1024)} %param.9), kind=kLoop, calls=%fused_computation.3 | loop fusion | flops 917504 | bytes 2756608 | tf_op jit(solution)/shard_map/transpose | solution.py:323
  3.3 0.0 copy-done.4
  3.3 0.6 broadcast_in_dim.2.asg_own
  3.9 0.0 copy-start.2
  3.9 0.0 copy-start
  3.9 80.1 %embed_and_assign.1 = (f32[256,1024]{1,0:T(8,128)}, f32[1024,448]{1,0:T(8,128)}, f32[8,1024]{1,0:T(8,128)}) custom-call(bf16[256,896]{1,0:T(8,128)(2,1)} %pooled_ref.1, bf16[896,3584]{1,0:T(8,128)(2,1)} %w_hbm.1, bf16[448,1024]{1,0:T(8,128)(2,1)} %fusion.cent_own, s32[8,256]{1,0:T(8,128)} %broadcast_in_dim.2.asg_own), custom_call_target="tpu_custom_call" | custom-call | tf_op jit(solution)/shard_map/embed_and_assign/pallas_call | solution.py:327
  84.0 0.8 slice_multiply_fusion
  84.8 0.0 copy-done.2
  84.8 0.0 copy-start.3
  84.8 0.0 copy-done
  84.8 1.8 %copy.9 = f32[1024,448]{1,0:T(8,128)} copy(f32[1024,448]{0,1:T(8,128)S(1)} %copy-done) | data formatting | bytes 3670016 | tf_op args[3]
  86.6 2.6 %divide_convert_fusion = (bf16[1024,448]{1,0:T(8,128)(2,1)S(1)}, f32[1024,448]{1,0:T(8,128)S(1)}) fusion(f32[1024]{0:T(1024)S(1)} %multiply_add_fusion.1, f32[1024,448]{1,0:T(8,128)} %get-tuple-element.8, f32[1024,448]{1,0:T(8,128)} %copy.9), kind=kLoop, calls=%fused_computation | loop fusion | flops 2293760 | bytes 6426624 | tf_op jit(solution)/shard_map/convert_element_type | solution.py:61
  89.2 0.0 copy-done.3
  89.2 1.7 %copy.10 = f32[1024,448]{0,1:T(8,128)} copy(f32[1024,448]{1,0:T(8,128)S(1)} %get-tuple-element.15) | data formatting | bytes 3670016
  91.0 0.0 copy-start.1
  91.0 1.3 %copy.11 = bf16[1024,448]{0,1:T(8,128)(2,1)} copy(bf16[1024,448]{1,0:T(8,128)(2,1)S(1)} %get-tuple-element.14) | data formatting | bytes 1835008
  92.2 0.0 copy-done.1
  92.2 1.0 %copy.13 = f32[256,1024]{1,0:T(8,128)} copy(f32[256,1024]{1,0:T(8,128)S(1)} %copy-done.1) | data formatting | bytes 2097152
  (1 shorter events, 0.0 us)
Async XLA Ops:
  0.6 2.7 %copy-start.4 = (s32[256]{0:T(256)S(1)}, s32[256]{0:T(256)}, u32[]{:S(2)}) copy-start(s32[256]{0:T(256)} %param.7) | copy-start | bytes 3076
  3.9 80.9 %copy-start.2 = (f32[1024]{0:T(1024)S(1)}, f32[1024]{0:T(1024)}, u32[]{:S(2)}) copy-start(f32[1024]{0:T(1024)} %param.9) | copy-start | bytes 12292
  3.9 80.9 %copy-start = (f32[1024,448]{0,1:T(8,128)S(1)}, f32[1024,448]{0,1:T(8,128)}, u32[]{:S(2)}) copy-start(f32[1024,448]{0,1:T(8,128)} %param.8) | copy-start | bytes 5505028
  84.8 4.4 %copy-start.3 = (f32[1024]{0:T(1024)}, f32[1024]{0:T(1024)S(1)}, u32[]{:S(2)}) copy-start(f32[1024]{0:T(1024)S(1)} %multiply_add_fusion.1) | copy-start | bytes 12292
  91.0 1.3 %copy-start.1 = (f32[256,1024]{1,0:T(8,128)S(1)}, f32[256,1024]{1,0:T(8,128)}, u32[]{:S(2)}) copy-start(f32[256,1024]{1,0:T(8,128)} %get-tuple-element.20) | copy-start | bytes 3145732

commit v3 on v2

--- a/solution.py
+++ b/solution.py
@@ -12,6 +12,8 @@
 EMA_DECAY = 0.9
 BF = jnp.bfloat16
 F32 = jnp.float32
+BLOCKS = 4
+PIECES = 2
 
 
 def plain_body(pooled, w_out, assignments, ema_sums, ema_counts):
@@ -63,17 +65,19 @@
 
 
 def kernel(
-    pooled_ref, w_hbm, cent_own, asg_own,
+    pooled_ref, w_hbm, ema_ref, ema_counts_ref, asg_own,
     dist_ref, sums_ref, counts_ref,
-    w_ref, pf, outgoing, incoming, embf, own, cent, asg, onehot,
+    cent_own, w_ref, pf, outgoing, incoming, embf, own, cent, asg, onehot,
     w_sem, cs, cr, as_, ar, zs, zr, gs, gr, es, er,
 ):
     d = lax.axis_index("dp")
     m = lax.axis_index("mp")
     docs = pooled_ref.shape[0]
-    quarter = docs // 4
+    block = docs // (2 * BLOCKS)
     dim = w_ref.shape[1]
     chunk = dim // 4
+    wide = dim // PIECES
+    heads = 8 // PIECES
     feats, centers = cent_own.shape
     half = feats // 2
     core, xi, yi = d % 2, (d // 2) % 2, d // 4
@@ -97,13 +101,17 @@
     def cols(c):
         return pl.ds(c * chunk, chunk)
 
+    def pieces(c):
+        return pl.ds(c * wide, wide)
+
     def rows(flow, i):
-        return pl.ds(pl.multiple_of((flow * 2 + i) * quarter, quarter), quarter)
+        return pl.ds(pl.multiple_of((i * 2 + flow) * block, block), block)
 
     w_copies = []
     for c in range(4):
         w_copies.append(pltpu.make_async_copy(w_hbm.at[:, cols(c)], w_ref.at[:, cols(c)], w_sem.at[c]))
         w_copies[c].start()
+    cent_own[...] = (ema_ref[...] / ema_counts_ref[0:1, :]).astype(BF)
 
     barrier = pltpu.get_barrier_semaphore()
     for k in range(1, 8):
@@ -143,29 +151,29 @@
         asg_copies[k] = go(remote(asg_own, asg.at[d], as_.at[k], ar.at[k], partner(k), m))
 
     def sum_copy(flow, i, c, to):
-        at = (flow, pl.ds(i * quarter, quarter), cols(c))
+        at = (flow, pl.ds(i * block, block), pieces(c))
         return remote(outgoing.at[at], incoming.at[at], zs.at[flow, i, c], zr.at[flow, i, c], d, to)
 
     def put(flow, i, c, value):
-        outgoing[flow, pl.ds(i * quarter, quarter), cols(c)] = value.astype(BF)
+        outgoing[flow, pl.ds(i * block, block), pieces(c)] = value.astype(BF)
 
     def arrived(flow, i, c):
-        return pf[rows(flow, i), cols(c)] + incoming[flow, pl.ds(i * quarter, quarter), cols(c)].astype(F32)
+        return pf[rows(flow, i), pieces(c)] + incoming[flow, pl.ds(i * block, block), pieces(c)].astype(F32)
+
+    def begin(i, c):
+        @pl.when(inner == 0)
+        def _():
+            put(near, i, c, pf[rows(near, i), pieces(c)])
+            sum_copy(near, i, c, ahead).start()
 
     for c in range(4):
         w_copies[c].wait()
         pf[:, cols(c)] = jnp.dot(pooled_ref[...], w_ref[:, cols(c)], preferred_element_type=F32)
-
-        @pl.when(inner == 0)
-        def _():
-            put(near, 0, c, pf[rows(near, 0), cols(c)])
-            sum_copy(near, 0, c, ahead).start()
-
-    @pl.when(inner == 0)
-    def _():
-        for c in range(4):
-            put(near, 1, c, pf[rows(near, 1), cols(c)])
-            sum_copy(near, 1, c, ahead).start()
+        if (c + 1) % (4 // PIECES) == 0:
+            begin(0, c // (4 // PIECES))
+    for i in range(1, BLOCKS):
+        for c in range(PIECES):
+            begin(i, c)
 
     def sum_near(i, c):
         @pl.when(inner == 1)
@@ -184,10 +192,10 @@
 
         @pl.when(inner == 0)
         def _():
-            pf[rows(far, i), cols(c)] = arrived(far, i, c)
+            pf[rows(far, i), pieces(c)] = arrived(far, i, c)
 
     def emb_copy(flow, i, b, to):
-        ref = embf.at[pl.ds(2 * b, 2), rows(flow, i), :]
+        ref = embf.at[pl.ds(heads * b, heads), rows(flow, i), :]
         return remote(ref, ref, gs.at[flow, i, b], gr.at[flow, i, b], d, to)
 
     def embed(i):
@@ -198,7 +206,7 @@
             value = value * inverse
             for b in range(8):
                 embf[b, rows(far, i), :] = value[:, b * feats:(b + 1) * feats].astype(BF)
-            for b in range(4):
+            for b in range(PIECES):
                 emb_copy(far, i, b, ahead).start()
 
     def emb_near(i, b):
@@ -222,96 +230,102 @@
                 embf.at[partner(k), rows(flow, i), :], own.at[d, rows(flow, i), :],
                 es.at[flow, i, k], er.at[flow, i, k], partner(k), m))
 
-    for t in range(5):
-        if t < 4:
-            sum_near(0, t)
-        if t >= 1:
-            sum_far(0, t - 1)
-    embed(0)
-    c_x[0].wait_recv()
-    c_rx = go(remote(half_slot(XN, 0), half_slot(XN, 0), cs.at[5], cr.at[5], YN, m))
-    c_y[1].wait_recv()
-    c_ry = go(remote(half_slot(YN, 1), half_slot(YN, 1), cs.at[6], cr.at[6], XN, m))
-    for t in range(7):
-        if t < 4:
-            sum_near(1, t)
-        if 1 <= t < 5:
-            sum_far(1, t - 1)
-        if t == 4:
-            embed(1)
-        if 2 <= t < 6:
-            emb_near(0, t - 2)
-        if 3 <= t:
-            emb_far(0, t - 3)
-    scatter("far", far, 0)
-    scatter("near", near, 0)
-    c_x[1].wait_recv()
-    c_px = go(remote(slot(XN), slot(XN), cs.at[7], cr.at[7], PC, m))
-    c_y[0].wait_recv()
-    c_py = go(remote(slot(YN), slot(YN), cs.at[8], cr.at[8], PC, m))
-    for t in range(5):
-        if t < 4:
-            emb_near(1, t)
-        if t >= 1:
-            emb_far(1, t - 1)
-    scatter("far", far, 1)
-    scatter("near", near, 1)
-    c_rx.wait_recv()
-    c_pd0 = go(remote(half_slot(DG, 0), half_slot(DG, 0), cs.at[9], cr.at[9], PC, m))
-    c_ry.wait_recv()
-    c_pd1 = go(remote(half_slot(DG, 1), half_slot(DG, 1), cs.at[10], cr.at[10], PC, m))
-
-    first_center = m * centers
-    ids = first_center + lax.broadcasted_iota(jnp.int32, (centers, docs), 0)
-    counts = jnp.zeros((8, centers), F32)
-    for k in range(8):
+    def mark(k):
         if k:
             asg_copies[k].wait_recv()
             row = asg[partner(k)][0:1, :]
         else:
             row = asg_own[0:1, :]
-        onehot[k] = jnp.where(ids == row, 1.0, 0.0).astype(BF)
-        counts = counts + lax.dot_general(
-            jnp.ones((8, docs), BF), onehot[k], (((1,), (1,)), ((), ())), preferred_element_type=F32)
-    counts_ref[...] = counts
-
+        column = jnp.broadcast_to(row, (128, docs)).T
+        for j in range(centers // 128):
+            ids = m * centers + j * 128 + lax.broadcasted_iota(jnp.int32, (docs, 128), 1)
+            onehot[k, :, j * 128:(j + 1) * 128] = jnp.where(ids == column, 1.0, 0.0).astype(BF)
+        count = jnp.dot(jnp.ones((8, docs), BF), onehot[k], preferred_element_type=F32)
+        counts_ref[...] = counts_ref[...] + count if k else count
+
+    norms = []
+    waits = {1: lambda: (c_p,), 3: lambda: (c_px,), 5: lambda: (c_py,), 7: lambda: (c_pd0, c_pd1)}
+
+    def product(h, k):
+        if h == 0 and k in waits:
+            for copy in waits[k]():
+                copy.wait_recv()
+        piece = slot(partner(k))[...] if k else cent_own[...]
+        if h == 0:
+            full = piece.astype(F32)
+            norms.append(jnp.sum(full * full, axis=0, keepdims=True))
+        these = pl.ds(h * (docs // 2), docs // 2)
+        value = jnp.dot(embf[partner(k), these, :], piece, preferred_element_type=F32)
+        dist_ref[these, :] = dist_ref[these, :] + value if k else value
+
+    def gather(i):
+        for b in range(PIECES):
+            emb_near(i, b)
+        scatter("far", far, i)
+        for b in range(PIECES):
+            emb_far(i, b)
+        scatter("near", near, i)
+
+    for i in range(BLOCKS):
+        for c in range(PIECES):
+            sum_near(i, c)
+        mark(2 * i)
+        for c in range(PIECES):
+            sum_far(i, c)
+        embed(i)
+        mark(2 * i + 1)
+        if i == 0:
+            c_x[0].wait_recv()
+            c_rx = go(remote(half_slot(XN, 0), half_slot(XN, 0), cs.at[5], cr.at[5], YN, m))
+            c_y[1].wait_recv()
+            c_ry = go(remote(half_slot(YN, 1), half_slot(YN, 1), cs.at[6], cr.at[6], XN, m))
+        if i >= 2:
+            gather(i - 2)
+    c_x[1].wait_recv()
+    c_px = go(remote(slot(XN), slot(XN), cs.at[7], cr.at[7], PC, m))
+    c_y[0].wait_recv()
+    c_py = go(remote(slot(YN), slot(YN), cs.at[8], cr.at[8], PC, m))
+    for k in (0, 2, 4):
+        product(0, k)
+    gather(2)
+    c_rx.wait_recv()
+    c_pd0 = go(remote(half_slot(DG, 0), half_slot(DG, 0), cs.at[9], cr.at[9], PC, m))
+    c_ry.wait_recv()
+    c_pd1 = go(remote(half_slot(DG, 1), half_slot(DG, 1), cs.at[10], cr.at[10], PC, m))
+    for k in (6, 1, 3):
+        product(0, k)
+    gather(3)
+    for k in (5, 7):
+        product(0, k)
+    for k in range(8):
+        product(1, k)
     doc_norms = jnp.zeros((docs, 1), F32)
     for b in range(8):
-        wide = embf[b].astype(F32)
-        doc_norms = doc_norms + jnp.sum(wide * wide, axis=1, keepdims=True)
-    norms = jnp.zeros((1, centers), F32)
-    waits = {1: (c_p,), 3: (c_px,), 5: (c_py,), 7: (c_pd0, c_pd1)}
-    for k in (0, 2, 4, 6, 1, 3, 5, 7):
-        for copy in waits.get(k, ()):
-            copy.wait_recv()
-        block = slot(partner(k))[...] if k else cent_own[...]
-        wide = block.astype(F32)
-        norms = norms + jnp.sum(wide * wide, axis=0, keepdims=True)
-        product = jnp.dot(embf[partner(k)], block, preferred_element_type=F32)
-        if k == 0:
-            dist_ref[...] = product
-        elif k < 7:
-            dist_ref[...] += product
-        else:
-            dist_ref[...] = doc_norms + norms - 2.0 * (dist_ref[...] + product)
-
-    sums_ref[...] = jnp.dot(onehot[0], embf[d], preferred_element_type=F32)
+        full = embf[b].astype(F32)
+        doc_norms = doc_norms + jnp.sum(full * full, axis=1, keepdims=True)
+    dist_ref[...] = doc_norms + sum(norms) - 2.0 * dist_ref[...]
+
+    def add(k, columns):
+        value = lax.dot_general(columns, onehot[k], (((0,), (0,)), ((), ())), preferred_element_type=F32)
+        sums_ref[...] = sums_ref[...] + value if k else value
+
+    add(0, embf[d])
     for k in (1, 2, 4, 6, 3, 5, 7):
-        for i in range(2):
+        for i in range(BLOCKS):
             for name in ("far", "near"):
                 e_copies[(name, i, k)].wait_recv()
-        sums_ref[...] += jnp.dot(onehot[k], own[partner(k)], preferred_element_type=F32)
+        add(k, own[partner(k)])
     for copy in sends:
         copy.wait_send()
-    for i in range(2):
-        for c in range(4):
+    for i in range(BLOCKS):
+        for c in range(PIECES):
             sum_copy(near, i, c, ahead).wait_send()
             emb_copy(far, i, c, ahead).wait_send()
 
     @pl.when(inner == 1)
     def _():
-        for i in range(2):
-            for c in range(4):
+        for i in range(BLOCKS):
+            for c in range(PIECES):
                 sum_copy(far, i, c, behind).wait_send()
                 emb_copy(near, i, c, behind).wait_send()
 
@@ -320,7 +334,6 @@
     docs, depth = pooled.shape
     dim = w_out.shape[1]
     centers, feats = ema_sums.shape
-    cent = (ema_sums / ema_counts[:, None]).astype(BF).T
     asg8 = jnp.broadcast_to(assignments[None, :], (8, docs))
     vmem = pl.BlockSpec(memory_space=pltpu.VMEM)
     dma = pltpu.SemaphoreType.DMA
@@ -328,12 +341,13 @@
         kernel,
         out_shape=(
             jax.ShapeDtypeStruct((docs, centers), F32),
-            jax.ShapeDtypeStruct((centers, feats), F32),
+            jax.ShapeDtypeStruct((feats, centers), F32),
             jax.ShapeDtypeStruct((8, centers), F32),
         ),
-        in_specs=[vmem, pl.BlockSpec(memory_space=pl.ANY), vmem, vmem],
+        in_specs=[vmem, pl.BlockSpec(memory_space=pl.ANY), vmem, vmem, vmem],
         out_specs=(vmem, vmem, vmem),
         scratch_shapes=[
+            pltpu.VMEM((feats, centers), BF),
             pltpu.VMEM((depth, dim), BF),
             pltpu.VMEM((docs, dim), F32),
             pltpu.VMEM((2, docs // 2, dim), BF),
@@ -342,15 +356,16 @@
             pltpu.VMEM((8, docs, feats), BF),
             pltpu.VMEM((8 * feats, centers), BF),
             pltpu.VMEM((8, 8, docs), jnp.int32),
-            pltpu.VMEM((8, centers, docs), BF),
-            dma((4,)), dma((11,)), dma((11,)), dma((8,)), dma((8,)), dma((2, 2, 4)), dma((2, 2, 4)),
-            dma((2, 2, 4)), dma((2, 2, 4)), dma((2, 2, 8)), dma((2, 2, 8)),
+            pltpu.VMEM((8, docs, centers), BF),
+            dma((4,)), dma((11,)), dma((11,)), dma((8,)), dma((8,)),
+            dma((2, BLOCKS, PIECES)), dma((2, BLOCKS, PIECES)), dma((2, BLOCKS, PIECES)), dma((2, BLOCKS, PIECES)),
+            dma((2, BLOCKS, 8)), dma((2, BLOCKS, 8)),
         ],
         compiler_params=pltpu.CompilerParams(
             collective_id=0, has_side_effects=True, vmem_limit_bytes=60 * 1024 * 1024),
         name="embed_and_assign",
-    )(pooled, w_out, cent, asg8)
-    return finish(distances, batch_sums, counts[0], ema_sums, ema_counts)
+    )(pooled, w_out, ema_sums.T, ema_counts[None, :], asg8)
+    return finish(distances, batch_sums.T, counts[0], ema_sums, ema_counts)
 
 
 def solution(mesh):

time: 93.5 us -> 88.5 us (0.947)
  local copies, waits for them, and re-layouts: 6.41 us -> 2.27 us
  other arithmetic: 6.01 us -> 4.52 us
    unnamed x14 -> x9, local copies, waits for them, and re-layouts: 5.81 us -> 0.99 us
    transpose x1 -> x0, other arithmetic: 2.64 us -> none  [fast_body(): cent = (ema_sums / ema_counts[:, None]).astype(BF).T]
    convert_element_type x1, other arithmetic: 2.6 us -> 3.76 us  [finish(): new_centroids = (new_sums / new_counts[:, None]).astype(BF)]
where the time goes in v3:
time: 88.5 us; the launch traced here: 88.2 us
  Pallas kernels  80.8 us (91%)
  other arithmetic  4.52 us (5%)
  local copies, waits for them, and re-layouts  2.27 us (3%)
    pallas_call x1, Pallas kernels, fast_body(): pl.pallas_call(kernel, out_shape=(jax.ShapeDtypeStruct((docs, centers), F...  80.8 us
    convert_element_type x1, other arithmetic, finish(): new_centroids = (new_sums / new_counts[:, None]).astype(BF)  3.76 us

profile of v3, /device:TPU:0, one launch (start us, length us, event | category | flops | bytes accessed | tf_op | source)
XLA Modules:
  0.0 88.2 jit_solution(12971622493070882480)
XLA Ops:
  0.6 1.3 %broadcast_in_dim.5.asg_own = s32[8,256]{1,0:T(8,128)} broadcast(s32[256]{0:T(256)} %param.7), dimensions={1} | broadcast | bytes 9216 | tf_op jit(solution)/shard_map/broadcast_in_dim | solution.py:337
  1.9 0.0 copy-start.2
  1.9 0.0 copy-start
  1.9 80.8 %embed_and_assign.1 = (f32[256,1024]{1,0:T(8,128)}, f32[448,1024]{1,0:T(8,128)}, f32[8,1024]{1,0:T(8,128)}) custom-call(bf16[256,896]{1,0:T(8,128)(2,1)} %pooled_ref.1, bf16[896,3584]{1,0:T(8,128)(2,1)} %w_hbm.1, f32[448,1024]{1,0:T(8,128)} %bitcast.6, f32[1,1024]{1,0:T(1,128)} %bitcast.7, s32[8,256]{1,0:T(8,128)} %broadcast_in_dim.5.asg_own), custom_call_target="tpu_custom_call" | custom-call | tf_op jit(solution)/shard_map/embed_and_assign/pallas_call | solution.py:340
  82.7 0.8 slice_multiply_fusion
  83.4 0.0 copy-done.2
  83.5 0.0 copy-done
  83.5 0.0 copy-start.3
  83.5 0.0 copy-start.1
  83.5 3.8 %divide_convert_fusion = (bf16[1024,448]{0,1:T(8,128)(2,1)}, f32[1024,448]{0,1:T(8,128)}) fusion(f32[1024]{0:T(1024)S(1)} %multiply_add_fusion, f32[448,1024]{1,0:T(8,128)} %get-tuple-element.8, f32[1024,448]{0,1:T(8,128)S(1)} %copy-done), kind=kLoop, calls=%fused_computation.1 | loop fusion | flops 2293760 | bytes 6426624 | tf_op jit(solution)/shard_map/convert_element_type | solution.py:63
  87.2 0.0 copy-done.3
  87.2 0.0 copy-done.1
  87.2 1.0 %copy.10 = f32[256,1024]{1,0:T(8,128)} copy(f32[256,1024]{1,0:T(8,128)S(1)} %copy-done.1) | data formatting | bytes 2097152
  (1 shorter events, 0.0 us)
Async XLA Ops:
  1.9 81.5 %copy-start.2 = (f32[1024]{0:T(1024)S(1)}, f32[1024]{0:T(1024)}, u32[]{:S(2)}) copy-start(f32[1024]{0:T(1024)} %param.9) | copy-start | bytes 12292
  1.9 81.5 %copy-start = (f32[1024,448]{0,1:T(8,128)S(1)}, f32[1024,448]{0,1:T(8,128)}, u32[]{:S(2)}) copy-start(f32[1024,448]{0,1:T(8,128)} %param.8) | copy-start | bytes 5505028
  83.5 3.8 %copy-start.3 = (f32[1024]{0:T(1024)}, f32[1024]{0:T(1024)S(1)}, u32[]{:S(2)}) copy-start(f32[1024]{0:T(1024)S(1)} %multiply_add_fusion) | copy-start | bytes 12292
  83.5 3.8 %copy-start.1 = (f32[256,1024]{1,0:T(8,128)S(1)}, f32[256,1024]{1,0:T(8,128)}, u32[]{:S(2)}) copy-start(f32[256,1024]{1,0:T(8,128)} %get-tuple-element.16) | copy-start | bytes 3145732

commit v4 on v3

--- a/solution.py
+++ b/solution.py
@@ -215,12 +215,16 @@
             emb_copy(far, i, b, ahead).wait_recv()
             emb_copy(far, i, b, ahead).start()
 
-    def emb_far(i, b):
-        emb_copy(near, i, b, behind).wait_recv()
-
+    def emb_far_inner(i, b):
         @pl.when(inner == 1)
         def _():
+            emb_copy(near, i, b, behind).wait_recv()
             emb_copy(near, i, b, behind).start()
+
+    def emb_far_end(i, b):
+        @pl.when(inner == 0)
+        def _():
+            emb_copy(near, i, b, behind).wait_recv()
 
     e_copies = {}
 
@@ -258,43 +262,49 @@
         value = jnp.dot(embf[partner(k), these, :], piece, preferred_element_type=F32)
         dist_ref[these, :] = dist_ref[these, :] + value if k else value
 
-    def gather(i):
-        for b in range(PIECES):
-            emb_near(i, b)
-        scatter("far", far, i)
-        for b in range(PIECES):
-            emb_far(i, b)
-        scatter("near", near, i)
-
-    for i in range(BLOCKS):
-        for c in range(PIECES):
-            sum_near(i, c)
-        mark(2 * i)
-        for c in range(PIECES):
-            sum_far(i, c)
-        embed(i)
-        mark(2 * i + 1)
-        if i == 0:
+    pieces_all = BLOCKS * PIECES
+    at_end = 11
+    for s in range(pieces_all + at_end):
+        if s < pieces_all:
+            sum_near(s // PIECES, s % PIECES)
+        n = s - 2
+        if 0 <= n < pieces_all:
+            sum_far(n // PIECES, n % PIECES)
+            if n % PIECES == PIECES - 1:
+                embed(n // PIECES)
+        n = s - 7
+        if 0 <= n < pieces_all:
+            emb_near(n // PIECES, n % PIECES)
+            if n % PIECES == PIECES - 1:
+                scatter("far", far, n // PIECES)
+        n = s - 9
+        if 0 <= n < pieces_all:
+            emb_far_inner(n // PIECES, n % PIECES)
+        n = s - at_end
+        if 0 <= n < pieces_all:
+            emb_far_end(n // PIECES, n % PIECES)
+            if n % PIECES == PIECES - 1:
+                scatter("near", near, n // PIECES)
+        if s < 8:
+            mark(s)
+        if s == 4:
             c_x[0].wait_recv()
             c_rx = go(remote(half_slot(XN, 0), half_slot(XN, 0), cs.at[5], cr.at[5], YN, m))
             c_y[1].wait_recv()
             c_ry = go(remote(half_slot(YN, 1), half_slot(YN, 1), cs.at[6], cr.at[6], XN, m))
-        if i >= 2:
-            gather(i - 2)
-    c_x[1].wait_recv()
-    c_px = go(remote(slot(XN), slot(XN), cs.at[7], cr.at[7], PC, m))
-    c_y[0].wait_recv()
-    c_py = go(remote(slot(YN), slot(YN), cs.at[8], cr.at[8], PC, m))
-    for k in (0, 2, 4):
-        product(0, k)
-    gather(2)
-    c_rx.wait_recv()
-    c_pd0 = go(remote(half_slot(DG, 0), half_slot(DG, 0), cs.at[9], cr.at[9], PC, m))
-    c_ry.wait_recv()
-    c_pd1 = go(remote(half_slot(DG, 1), half_slot(DG, 1), cs.at[10], cr.at[10], PC, m))
-    for k in (6, 1, 3):
-        product(0, k)
-    gather(3)
+        if s == 11:
+            c_x[1].wait_recv()
+            c_px = go(remote(slot(XN), slot(XN), cs.at[7], cr.at[7], PC, m))
+            c_y[0].wait_recv()
+            c_py = go(remote(slot(YN), slot(YN), cs.at[8], cr.at[8], PC, m))
+        if s == 15:
+            c_rx.wait_recv()
+            c_pd0 = go(remote(half_slot(DG, 0), half_slot(DG, 0), cs.at[9], cr.at[9], PC, m))
+            c_ry.wait_recv()
+            c_pd1 = go(remote(half_slot(DG, 1), half_slot(DG, 1), cs.at[10], cr.at[10], PC, m))
+        if s >= 14:
+            product(0, {14: 0, 15: 2, 16: 4, 17: 6, 18: 1}[s])
+    product(0, 3)
     for k in (5, 7):
         product(0, k)
     for k in range(8):

time: 88.5 us -> 86.4 us (0.976)
  Pallas kernels: 80.8 us -> 78.7 us
    pallas_call x1, Pallas kernels: 80.8 us -> 78.7 us  [fast_body(): pl.pallas_call(kernel, out_shape=(jax.ShapeDtypeStruct((docs, centers), F...]
where the time goes in v4:
time: 86.4 us; the launch traced here: 86.2 us
  Pallas kernels  78.7 us (91%)
  other arithmetic  4.52 us (5%)
  local copies, waits for them, and re-layouts  2.27 us (3%)
    pallas_call x1, Pallas kernels, fast_body(): pl.pallas_call(kernel, out_shape=(jax.ShapeDtypeStruct((docs, centers), F...  78.7 us
    convert_element_type x1, other arithmetic, finish(): new_centroids = (new_sums / new_counts[:, None]).astype(BF)  3.76 us

profile of v4, /device:TPU:0, one launch (start us, length us, event | category | flops | bytes accessed | tf_op | source)
XLA Modules:
  0.0 86.2 jit_solution(14688994078779549936)
XLA Ops:
  0.6 1.3 %broadcast_in_dim.5.asg_own = s32[8,256]{1,0:T(8,128)} broadcast(s32[256]{0:T(256)} %param.7), dimensions={1} | broadcast | bytes 9216 | tf_op jit(solution)/shard_map/broadcast_in_dim | solution.py:347
  1.9 0.0 copy-start.2
  1.9 0.0 copy-start
  1.9 78.7 %embed_and_assign.1 = (f32[256,1024]{1,0:T(8,128)}, f32[448,1024]{1,0:T(8,128)}, f32[8,1024]{1,0:T(8,128)}) custom-call(bf16[256,896]{1,0:T(8,128)(2,1)} %pooled_ref.1, bf16[896,3584]{1,0:T(8,128)(2,1)} %w_hbm.1, f32[448,1024]{1,0:T(8,128)} %bitcast.6, f32[1,1024]{1,0:T(1,128)} %bitcast.7, s32[8,256]{1,0:T(8,128)} %broadcast_in_dim.5.asg_own), custom_call_target="tpu_custom_call" | custom-call | tf_op jit(solution)/shard_map/embed_and_assign/pallas_call | solution.py:350
  80.6 0.8 slice_multiply_fusion
  81.4 0.0 copy-done.2
  81.4 0.0 copy-done
  81.4 0.0 copy-start.3
  81.4 0.0 copy-start.1
  81.4 3.8 %divide_convert_fusion = (bf16[1024,448]{0,1:T(8,128)(2,1)}, f32[1024,448]{0,1:T(8,128)}) fusion(f32[1024]{0:T(1024)S(1)} %multiply_add_fusion, f32[448,1024]{1,0:T(8,128)} %get-tuple-element.8, f32[1024,448]{0,1:T(8,128)S(1)} %copy-done), kind=kLoop, calls=%fused_computation.1 | loop fusion | flops 2293760 | bytes 6426624 | tf_op jit(solution)/shard_map/convert_element_type | solution.py:63
  85.2 0.0 copy-done.3
  85.2 0.0 copy-done.1
  85.2 1.0 %copy.10 = f32[256,1024]{1,0:T(8,128)} copy(f32[256,1024]{1,0:T(8,128)S(1)} %copy-done.1) | data formatting | bytes 2097152
  (1 shorter events, 0.0 us)
Async XLA Ops:
  1.9 79.5 %copy-start.2 = (f32[1024]{0:T(1024)S(1)}, f32[1024]{0:T(1024)}, u32[]{:S(2)}) copy-start(f32[1024]{0:T(1024)} %param.9) | copy-start | bytes 12292
  1.9 79.5 %copy-start = (f32[1024,448]{0,1:T(8,128)S(1)}, f32[1024,448]{0,1:T(8,128)}, u32[]{:S(2)}) copy-start(f32[1024,448]{0,1:T(8,128)} %param.8) | copy-start | bytes 5505028
  81.4 3.8 %copy-start.3 = (f32[1024]{0:T(1024)}, f32[1024]{0:T(1024)S(1)}, u32[]{:S(2)}) copy-start(f32[1024]{0:T(1024)S(1)} %multiply_add_fusion) | copy-start | bytes 12292
  81.4 3.8 %copy-start.1 = (f32[256,1024]{1,0:T(8,128)S(1)}, f32[256,1024]{1,0:T(8,128)}, u32[]{:S(2)}) copy-start(f32[256,1024]{1,0:T(8,128)} %get-tuple-element.16) | copy-start | bytes 3145732
